TPU v7x, 128 devices: a whole 4x4x4 slice. The times are simulated.
128 devices in a mesh: req: 16 (over x, y), mlp: 8 (over z, core).
Axes of the slice: x: 4, y: 4, z: 4, core: 2. Of those that a mesh axis runs over, the one named last changes fastest.
Arguments:
- tokens: bfloat16 [4096, 2048], P(('req', 'mlp')), may hold values from -6 to 6
- cached_states: float32 [256, 8, 256, 512], P('req', 'mlp'), may hold values from -12 to 12
- prompt_lengths: int32 [256], P('req'), may hold values from 1 to 4096, as said below
- accepted: int32 [256], P('req'), may hold values from 1 to 16, as said below
- owner_slot: int32 [256], P('req'), may hold values from 0 to 255, as said below
- w_query: bfloat16 [2048, 2048], P(None, 'mlp'), may hold values from -0.125 to 0.125
- w_key: bfloat16 [2048, 2048], P(None, 'mlp'), may hold values from -0.125 to 0.125
- w_value: bfloat16 [2048, 4096], P(None, 'mlp'), may hold values from -0.125 to 0.125
- w_gate_ret: bfloat16 [2048, 4096], P(None, 'mlp'), may hold values from -0.125 to 0.125
- w_out: bfloat16 [4096, 2048], P('mlp'), may hold values from -0.09375 to 0.09375
- w_gate: bfloat16 [2048, 4096], P('req', 'mlp'), may hold values from -0.125 to 0.125
- w_up: bfloat16 [2048, 4096], P('req', 'mlp'), may hold values from -0.125 to 0.125
- w_down: bfloat16 [4096, 2048], P('mlp', 'req'), may hold values from -0.09375 to 0.09375
Outputs:
- mixed: bfloat16 [4096, 2048], P(('req', 'mlp'))
- new_states: float32 [256, 8, 256, 512], P('req', 'mlp')
Inputs may be any that keep to these rules, and one draw needn't show every extreme that they name: `prompt_lengths`: request r belongs to tenant k = (4 r) // 256, so the four tenants hold consecutive ranges of 64 requests; its prompt length is drawn evenly from 1 to 4^(k + 3). `accepted`: number of leading drafts of request r that are kept, drawn evenly for each request. A permutation of the requests; for request r on req block i = r // 16, owner_slot[r] = j * 16 + i + c with owner block j and 0 <= c < 1, and each pair (j, c) occurs exactly once within a block.
All inputs are finite; a program needn't handle non-finite values.
Results may differ from a plain program's by a relative error of at most 0.017.
Values may be sent and summed in bfloat16 or wider, within the bound.
No kernel may reach another device: no remote copies, remote signals or barrier semaphores. Data moves between devices by JAX's collectives and lax.ppermute only.
A program may use at most 128 MiB of HBM per device.

v0:
```python
import math
import jax
import jax.numpy as jnp
from jax import lax
from jax.sharding import PartitionSpec as P

DRAFT = 16
epsilon = 1e-05


def layer_norm(inputs):
    average = jnp.mean(inputs, axis=-1, keepdims=True)
    centred = inputs - average
    variance = jnp.mean(centred * centred, axis=-1, keepdims=True)
    return centred * lax.rsqrt(variance + epsilon)


def decays(head_count, first_head):
    head_index = jnp.arange(head_count, dtype=jnp.float32) + first_head
    return 1.0 - jnp.exp2(-5.0 - head_index)


def rotate(inputs, positions):
    half_width = inputs.shape[-1] // 2
    frequencies = jnp.exp(
        -math.log(10000.0) * jnp.arange(half_width, dtype=jnp.float32) / half_width
    )
    angles = positions[:, :, None] * frequencies[None, None, :]
    cosine_part = jnp.cos(angles)[:, :, None, :]
    sine_part = jnp.sin(angles)[:, :, None, :]
    front_half = inputs[..., :half_width]
    back_half = inputs[..., half_width:]
    return jnp.concatenate(
        [
            front_half * cosine_part - back_half * sine_part,
            front_half * sine_part + back_half * cosine_part,
        ],
        axis=-1,
    )


def state_weights(states, accepted, gammas, draft_count):
    draft_pos = jnp.arange(draft_count, dtype=jnp.float32)
    accepted_f = accepted.astype(jnp.float32)
    exponent = accepted_f[:, None, None] - 1.0 - draft_pos[None, None, :]
    draft_weights = jnp.where(
        exponent >= 0, jnp.power(gammas[None, :, None], jnp.maximum(exponent, 0.0)), 0.0
    )
    old_part = jnp.power(gammas[None, :], accepted_f[:, None])[:, :, None, None] * states
    return (old_part, draft_weights)


def fold_update(key_rows, values, draft_weights):
    scaled = key_rows.astype(jnp.float32) * jnp.transpose(draft_weights, (0, 2, 1))[..., None]
    return jnp.einsum(
        "rshd,rshv->rhdv", scaled, values.astype(jnp.float32), precision=lax.Precision.HIGHEST
    )


def retain_outputs(queries, key_rows, values, states, gammas):
    draft_count = queries.shape[1]
    draft_pos = jnp.arange(draft_count, dtype=jnp.float32)
    distance = draft_pos[:, None] - draft_pos[None, :]
    decay_mask = jnp.where(
        distance[None] >= 0, jnp.power(gammas[:, None, None], jnp.maximum(distance, 0.0)[None]), 0.0
    )
    scores = jnp.einsum("rthd,rshd->rhts", queries, key_rows, preferred_element_type=jnp.float32)
    weights = (scores * decay_mask[None]).astype(jnp.bfloat16)
    within = jnp.einsum("rhts,rshv->rthv", weights, values, preferred_element_type=jnp.float32)
    carried = jnp.einsum(
        "rthd,rhdv->rthv", queries.astype(jnp.float32), states, precision=lax.Precision.HIGHEST
    )
    carried = carried * jnp.power(gammas[None, None, :, None], draft_pos[None, :, None, None] + 1.0)
    return within + carried


def per_device(
    tokens,
    cached_states,
    prompt_lengths,
    accepted,
    owner_slot,
    w_query,
    w_key,
    w_value,
    w_gate_ret,
    w_out,
    w_gate,
    w_up,
    w_down,
):
    requests = cached_states.shape[0]
    heads_here = cached_states.shape[1]
    key_width = cached_states.shape[2]
    value_width = cached_states.shape[3]
    draft_count = DRAFT
    per_peer = requests // lax.axis_size("req")
    first_head = (lax.axis_index("mlp") * heads_here).astype(jnp.float32)
    gammas = decays(heads_here, first_head)
    target_pos = owner_slot // requests * per_peer + owner_slot % per_peer
    local_ids = jnp.arange(requests, dtype=jnp.int32)
    send_order = jnp.sum(
        jnp.where(target_pos[None, :] == local_ids[:, None], local_ids[None, :], 0), axis=1
    )
    old_part, draft_weights = state_weights(cached_states, accepted, gammas, draft_count)
    group_rows = lax.all_gather(tokens, "mlp", axis=0, tiled=True)
    row_count = group_rows.shape[0]
    normed = layer_norm(group_rows.astype(jnp.float32)).astype(jnp.bfloat16)
    queries = jnp.dot(normed, w_query, preferred_element_type=jnp.float32).reshape(
        requests, draft_count, heads_here, key_width
    )
    key_rows = (
        jnp.dot(normed, w_key, preferred_element_type=jnp.float32) * (1.0 / math.sqrt(key_width))
    ).reshape(requests, draft_count, heads_here, key_width)
    values = (
        jnp.dot(normed, w_value, preferred_element_type=jnp.float32)
        .astype(jnp.bfloat16)
        .reshape(requests, draft_count, heads_here, value_width)
    )
    gate_ret = jnp.dot(normed, w_gate_ret, preferred_element_type=jnp.float32).reshape(
        requests, draft_count, heads_here, value_width
    )
    positions = (
        prompt_lengths[:, None] + jnp.arange(draft_count, dtype=jnp.int32)[None, :]
    ).astype(jnp.float32)
    rotated_q = rotate(queries, positions).astype(jnp.bfloat16)
    rotated_k = rotate(key_rows, positions).astype(jnp.bfloat16)
    fresh = old_part + fold_update(rotated_k, values, draft_weights)
    new_states = lax.all_to_all(
        jnp.take(fresh, send_order, axis=0).astype(jnp.bfloat16),
        "req",
        split_axis=0,
        concat_axis=0,
        tiled=True,
    ).astype(jnp.float32)
    outputs = retain_outputs(rotated_q, rotated_k, values, cached_states, gammas)
    joined = (
        (layer_norm(outputs) * jax.nn.silu(gate_ret))
        .astype(jnp.bfloat16)
        .reshape(row_count, heads_here * value_width)
    )
    partials = jnp.dot(joined, w_out, preferred_element_type=jnp.float32)
    share = tokens.shape[0]
    summed = lax.psum(partials.astype(jnp.bfloat16), "mlp").astype(jnp.float32)
    residual = group_rows.astype(jnp.float32) + summed
    hidden_in = layer_norm(residual).astype(jnp.bfloat16)
    residual_share = lax.dynamic_slice_in_dim(residual, lax.axis_index("mlp") * share, share, 0)
    gate_sum = jnp.dot(
        hidden_in,
        lax.all_gather(w_gate, "req", axis=0, tiled=True),
        preferred_element_type=jnp.float32,
    )
    up_sum = jnp.dot(
        hidden_in,
        lax.all_gather(w_up, "req", axis=0, tiled=True),
        preferred_element_type=jnp.float32,
    )
    hidden = (jax.nn.silu(gate_sum) * up_sum).astype(jnp.bfloat16)
    down_terms = jnp.dot(
        hidden,
        lax.all_gather(w_down, "req", axis=1, tiled=True),
        preferred_element_type=jnp.float32,
    )
    mixed = (
        residual_share
        + lax.psum_scatter(
            down_terms.astype(jnp.bfloat16), "mlp", scatter_dimension=0, tiled=True
        ).astype(jnp.float32)
    ).astype(jnp.bfloat16)
    return (mixed, new_states)


def solution(mesh):
    return jax.shard_map(
        per_device,
        mesh=mesh,
        in_specs=(
            P(("req", "mlp"), None),
            P("req", "mlp", None, None),
            P("req"),
            P("req"),
            P("req"),
            P(None, "mlp"),
            P(None, "mlp"),
            P(None, "mlp"),
            P(None, "mlp"),
            P("mlp", None),
            P("req", "mlp"),
            P("req", "mlp"),
            P("mlp", "req"),
        ),
        out_specs=(P(("req", "mlp"), None), P("req", "mlp", None, None)),
        check_vma=False,
    )
```

profile of v0, /device:TPU:0, one launch (start us, length us, event | category | flops | bytes accessed | tf_op | source)
XLA Modules:
  0.0 292.6 jit_solution(9923239641830720972)
XLA Ops:
  8.0 0.0 copy-start
  8.0 0.0 copy-start.13
  8.0 0.0 all-gather.5.cloned.1.call-start
  8.1 0.7 all-gather.5.cloned.1.call-update
  8.8 0.0 all-reduce.2.cloned.1.call-start
  8.9 1.3 convert_add_fusion.1
  10.2 0.7 add_convert_fusion.1
  10.9 0.7 power_select_fusion
  11.6 25.0 %all-gather.5.cloned.1.call-done = bf16[256,2048]{1,0:T(8,128)(2,1)} async-done(((bf16[32,2048]{1,0:T(8,128)(2,1)}), bf16[256,2048]{1,0:T(8,128)(2,1)}) %all-gather.5.cloned.1.call-update) | async-done | bytes 1048592 | tf_op jit(solution)/shard_map/all_gather | solution.py:106
  36.6 1.6 convert_reduce_fusion
  38.3 0.0 copy-start.8
  38.3 2.0 fusion.7
  40.2 0.0 copy-done.13
  40.2 0.0 copy-start.10
  40.3 1.7 fusion.62
  42.0 2.0 convolution_multiply_fusion.1
  44.0 0.6 fusion.46
  44.6 0.0 copy-start.5
  44.6 0.0 copy-start.6
  44.7 0.6 copy-done.5
  45.3 0.0 copy-done.6
  45.3 0.0 copy-done.1
  45.3 3.7 %fusion.14 = f32[16,1,512,16]{2,3,0,1:T(8,128)} fusion(f32[16,1,256,512]{3,2,1,0:T(8,128)S(1)} %copy-done.1, f32[16]{0:T(128)S(1)} %add_power_fusion, bf16[16,16,128]{2,1,0:T(8,128)(2,1)S(1)} %get-tuple-element.10, bf16[16,16,128]{2,1,0:T(8,128)(2,1)S(1)} %get-tuple-element.11), kind=kOutput, calls=%fused_computation.25 | convolution fusion | flops 403046400 | bytes 9044032 | tf_op jit(solution)/shard_map/rthd,rhdv->rthv/dot_general | solution.py:70
  49.0 0.0 copy-done.8
  49.0 0.0 copy-done.10
  49.0 0.0 copy-done.2
  49.0 0.8 convolution_convert_fusion.2
  49.7 2.2 fusion.65
  52.0 1.2 multiply_reduce_fusion.1
  53.2 0.0 copy-start.3
  53.2 2.4 fusion.59
  55.7 0.0 copy-done.3
  55.7 0.2 multiply_convert_fusion.1
  55.9 0.0 copy-start.14
  56.0 1.7 convolution_convert_fusion.1
  57.7 0.0 all-reduce.2.cloned.1.call-update
  57.7 0.0 all-gather.7.cloned.1.call-start
  57.7 0.5 all-gather.7.cloned.1.call-update
  58.3 0.0 all-gather.9.cloned.1.call-start
  58.3 0.5 all-gather.9.cloned.1.call-update
  58.9 0.0 all-gather.11.cloned.1.call-start
  58.9 0.5 all-gather.11.cloned.1.call-update
  59.5 0.1 select_reduce_fusion
  59.6 0.5 compare_and_fusion
  60.1 0.0 copy-done.7
  60.1 8.5 %fusion.1 = bf16[16,256,512]{2,1,0:T(8,128)(2,1)} fusion(f32[16,1,256,512]{3,2,1,0:T(8,128)} %param.14, f32[16]{0:T(128)S(1)} %copy-done.9, bf16[16,16,512]{2,1,0:T(8,128)(2,1)S(1)} %bitcast.68, f32[16,16]{1,0:T(8,128)S(1)} %copy-done.7, bf16[16,16,128]{2,1,0:T(8,128)(2,1)S(1)} %get-tuple-element.7, bf16[16,16,128]{2,1,0:T(8,128)(2,1)S(1)} %get-tuple-element.6), kind=kOutput, calls=%fused_computation.4 | convolution fusion | flops 409272320 | bytes 12977216 | tf_op jit(solution)/shard_map/rshd,rshv->rhdv/dot_general | solution.py:55
  68.7 5.1 %gather_fusion = bf16[16,256,512]{2,1,0:T(8,128)(2,1)} fusion(bf16[16,256,512]{2,1,0:T(8,128)(2,1)} %fusion.1, s32[1024]{0:T(1024)S(1)} %pad_clamp_fusion), kind=kCustom, calls=%fused_computation | custom fusion | bytes 8388672 | tf_op jit(solution)/shard_map/jit(_take)/gather | solution.py:130
  73.7 5.5 %fusion.4 = bf16[16,1,256,512]{3,2,1,0:T(8,128)(2,1)} fusion(bf16[16,256,512]{2,1,0:T(8,128)(2,1)} %gather_fusion, pred[16]{0:T(512)(128)(4,1)S(1)} %copy-done.11), kind=kLoop, calls=%fused_computation.8 | loop fusion | flops 2097152 | bytes 8388624 | tf_op jit(solution)/shard_map/convert_element_type | solution.py:130
  79.2 6.9 %all-to-all-start = ((bf16[16,1,256,512]{3,2,1,0:T(8,128)(2,1)}), bf16[16,1,256,512]{3,2,1,0:T(8,128)(2,1)}, u32[]{:S(2)}, u32[]{:S(2)}) async-start(bf16[16,1,256,512]{3,2,1,0:T(8,128)(2,1)} %fusion.4), calls=%async_computation.1 | async-start | bytes 8388608 | tf_op jit(solution)/shard_map/all_to_all | solution.py:129
  86.1 0.2 reduce-scatter.2.cloned.1.call-start
  86.3 35.1 %all-reduce.2.cloned.1.call-done = bf16[256,2048]{1,0:T(8,128)(2,1)} async-done(((bf16[256,2048]{1,0:T(8,128)(2,1)}), bf16[256,2048]{1,0:T(8,128)(2,1)}) %all-reduce.2.cloned.1.call-update) | async-done | bytes 1048592 | tf_op jit(solution)/shard_map/psum | solution.py:144
  121.4 2.9 convert_add_fusion
  124.3 0.0 copy-done.4
  124.3 0.5 multiply_reduce_fusion
  124.8 18.6 %all-gather.7.cloned.1.call-done = bf16[2048,512]{1,0:T(8,128)(2,1)} async-done(((bf16[128,512]{1,0:T(8,128)(2,1)}), bf16[2048,512]{1,0:T(8,128)(2,1)}) %all-gather.7.cloned.1.call-update) | async-done | bytes 2097168 | tf_op jit(solution)/shard_map/all_gather | solution.py:150
  143.5 3.5 %fusion.58 = f32[256,512]{1,0:T(8,128)} fusion(bf16[2048,512]{1,0:T(8,128)(2,1)} %all-gather.7.cloned.1.call-done, f32[256]{0:T(256)S(1)} %add_rsqrt_fusion.1, f32[256]{0:T(256)S(1)} %broadcast_multiply_fusion.1, bf16[256,2048]{1,0:T(8,128)(2,1)} %all-reduce.2.cloned.1.call-done, bf16[256,2048]{1,0:T(8,128)(2,1)S(1)} %copy-done.2), kind=kOutput, calls=%fused_computation.101 | convolution fusion | flops 540016640 | bytes 4720640 | tf_op jit(solution)/shard_map/dot_general | solution.py:148
  147.0 51.2 %all-gather.9.cloned.1.call-done = bf16[2048,512]{1,0:T(8,128)(2,1)} async-done(((bf16[128,512]{1,0:T(8,128)(2,1)}), bf16[2048,512]{1,0:T(8,128)(2,1)}) %all-gather.9.cloned.1.call-update) | async-done | bytes 2097168 | tf_op jit(solution)/shard_map/all_gather | solution.py:155
  198.2 48.6 %all-gather.11.cloned.1.call-done = bf16[512,2048]{1,0:T(8,128)(2,1)} async-done(((bf16[512,128]{1,0:T(8,128)(2,1)}), bf16[512,2048]{1,0:T(8,128)(2,1)}) %all-gather.11.cloned.1.call-update) | async-done | bytes 2097168 | tf_op jit(solution)/shard_map/all_gather | solution.py:161
  246.8 5.2 %convolution_convert_fusion = bf16[256,2048]{1,0:T(8,128)(2,1)} fusion(bf16[512,2048]{1,0:T(8,128)(2,1)} %all-gather.11.cloned.1.call-done, bf16[2048,512]{1,0:T(8,128)(2,1)} %all-gather.9.cloned.1.call-done, f32[256,512]{1,0:T(8,128)} %fusion.58, f32[256]{0:T(256)S(1)} %add_rsqrt_fusion.1, f32[256]{0:T(256)S(1)} %broadcast_multiply_fusion.1, ...), kind=kOutput, calls=%fused_computation.12 | convolution fusion | flops 1078198272 | bytes 7866368 | tf_op jit(solution)/shard_map/dot_general | solution.py:159
  252.0 0.0 reduce-scatter.2.cloned.1.call-update
  252.0 0.0 all-to-all-done
  252.0 6.7 %convert_element_type.101 = f32[16,1,256,512]{3,2,1,0:T(8,128)} convert(bf16[16,1,256,512]{3,2,1,0:T(8,128)(2,1)} %all-to-all-done) | non-fusion elementwise | flops 2097152 | bytes 12582912 | tf_op jit(solution)/shard_map/convert_element_type | solution.py:135
  258.7 24.9 %reduce-scatter.2.cloned.1.call-done = bf16[32,2048]{1,0:T(8,128)(2,1)} async-done(((bf16[256,2048]{1,0:T(8,128)(2,1)}), bf16[32,2048]{1,0:T(8,128)(2,1)}) %reduce-scatter.2.cloned.1.call-update) | async-done | bytes 131088 | tf_op jit(solution)/shard_map/reduce_scatter | solution.py:166
  283.6 1.7 add_convert_fusion
  (23 shorter events, 0.1 us)
Async XLA Ops:
  8.0 47.9 %copy-start = (bf16[512,2048]{1,0:T(8,128)(2,1)S(1)}, bf16[512,2048]{1,0:T(8,128)(2,1)}, u32[]{:S(2)}) copy-start(bf16[512,2048]{1,0:T(8,128)(2,1)} %param.22) | copy-start | bytes 6291460
  8.0 32.2 %copy-start.13 = (bf16[2048,256]{1,0:T(8,128)(2,1)S(1)}, bf16[2048,256]{1,0:T(8,128)(2,1)}, u32[]{:S(2)}) copy-start(bf16[2048,256]{1,0:T(8,128)(2,1)} %param.18) | copy-start | bytes 3145732
  8.0 28.6 %all-gather.5.cloned.1.call-start = ((), (), s32[]{:S(2)}) async-start(), calls=%async_computation.2 | async-start | bytes 1179648 | tf_op jit(solution)/shard_map/all_gather | solution.py:106
  8.8 112.6 %all-reduce.2.cloned.1.call-start = ((), (), s32[]{:S(2)}) async-start(), calls=%async_computation.3 | async-start | bytes 2097152 | tf_op jit(solution)/shard_map/psum | solution.py:144
  36.6 8.6 %copy-start.1 = (f32[16,1,256,512]{3,2,1,0:T(8,128)S(1)}, f32[16,1,256,512]{3,2,1,0:T(8,128)}, u32[]{:S(2)}) copy-start(f32[16,1,256,512]{3,2,1,0:T(8,128)} %param.14) | copy-start | bytes 25165828
  38.3 10.7 %copy-start.8 = (f32[256]{0:T(256)}, f32[256]{0:T(256)S(1)}, u32[]{:S(2)}) copy-start(f32[256]{0:T(256)S(1)} %broadcast_multiply_fusion.2) | copy-start | bytes 3076
  40.2 8.7 %copy-start.10 = (f32[256]{0:T(256)}, f32[256]{0:T(256)S(1)}, u32[]{:S(2)}) copy-start(f32[256]{0:T(256)S(1)} %add_rsqrt_fusion.2) | copy-start | bytes 3076
  44.6 0.6 copy-start.5
  44.6 0.6 copy-start.6
  45.3 3.7 %copy-start.2 = (bf16[256,2048]{1,0:T(8,128)(2,1)S(1)}, bf16[256,2048]{1,0:T(8,128)(2,1)}, u32[]{:S(2)}) copy-start(bf16[256,2048]{1,0:T(8,128)(2,1)} %all-gather.5.cloned.1.call-done) | copy-start | bytes 3145732
  45.3 3.7 %copy-start.12 = (bf16[2048,512]{1,0:T(8,128)(2,1)S(1)}, bf16[2048,512]{1,0:T(8,128)(2,1)}, u32[]{:S(2)}) copy-start(bf16[2048,512]{1,0:T(8,128)(2,1)} %param.20) | copy-start | bytes 6291460
  53.2 2.4 copy-start.3
  55.9 3.5 %copy-start.14 = (s32[16]{0:T(128)S(1)}, s32[16]{0:T(128)}, u32[]{:S(2)}) copy-start(s32[16]{0:T(128)} %param.17) | copy-start | bytes 196
  55.9 4.2 %copy-start.7 = (f32[16,16]{1,0:T(8,128)S(1)}, f32[16,16]{1,0:T(8,128)}, u32[]{:S(2)}) copy-start(f32[16,16]{1,0:T(8,128)} %get-tuple-element.16) | copy-start | bytes 3076
  55.9 4.2 %copy-start.9 = (f32[16]{0:T(128)S(1)}, f32[16]{0:T(128)}, u32[]{:S(2)}) copy-start(f32[16]{0:T(128)} %get-tuple-element.13) | copy-start | bytes 196
  57.7 85.8 %all-gather.7.cloned.1.call-start = ((), (), s32[]{:S(2)}) async-start(), calls=%async_computation.4 | async-start | bytes 2228224 | tf_op jit(solution)/shard_map/all_gather | solution.py:150
  58.3 139.9 %all-gather.9.cloned.1.call-start = ((), (), s32[]{:S(2)}) async-start(), calls=%async_computation.5 | async-start | bytes 2228224 | tf_op jit(solution)/shard_map/all_gather | solution.py:155
  58.9 187.9 %all-gather.11.cloned.1.call-start = ((), (), s32[]{:S(2)}) async-start(), calls=%async_computation.6 | async-start | bytes 2228224 | tf_op jit(solution)/shard_map/all_gather | solution.py:161
  68.7 5.1 %copy-start.11 = (pred[16]{0:T(512)(128)(4,1)S(1)}, pred[16]{0:T(512)(128)(4,1)}, u32[]{:S(2)}) copy-start(pred[16]{0:T(512)(128)(4,1)} %compare_and_fusion) | copy-start | bytes 52
  79.2 172.8 %all-to-all-start = ((bf16[16,1,256,512]{3,2,1,0:T(8,128)(2,1)}), bf16[16,1,256,512]{3,2,1,0:T(8,128)(2,1)}, u32[]{:S(2)}, u32[]{:S(2)}) async-start(bf16[16,1,256,512]{3,2,1,0:T(8,128)(2,1)} %fusion.4), calls=%async_computation.1 | async-start | bytes 8388608 | tf_op jit(solution)/shard_map/all_to_all | solution.py:129
  86.1 197.5 %reduce-scatter.2.cloned.1.call-start = ((), (), s32[]{:S(2)}) async-start(), calls=%async_computation.7 | async-start | bytes 1179648 | tf_op jit(solution)/shard_map/reduce_scatter | solution.py:166
  121.4 2.9 copy-start.4
Sparse Core Ops, SparseCore 0:
  10.6 26.0 all-gather.4
  57.8 63.5 all-reduce.1
  252.1 31.4 reduce-scatter.1
Sparse Core Ops, SparseCore 1:
  60.3 83.1 all-gather.6
  145.5 52.7 all-gather.8
  200.2 46.5 all-gather.10
where the time goes:
time: 293 us
  waiting for transfers between devices  206 us (70%)
  matrix products  31.8 us (11%)
  other arithmetic  26.4 us (9%)
  between operations  15.7 us (5%)
  starting transfers between devices  7.29 us (2%)
  local copies, waits for them, and re-layouts  5.76 us (2%)
    all_gather x1, waiting for transfers between devices, per_device(): lax.all_gather(w_up, 'req', axis=0, tiled=True)  51.2 us
    all_gather x1, waiting for transfers between devices, per_device(): lax.all_gather(w_down, 'req', axis=1, tiled=True)  48.6 us
    psum x1, waiting for transfers between devices, per_device(): summed = lax.psum(partials.astype(jnp.bfloat16), 'mlp').astype(jnp.float32)  35.1 us
    all_gather x1, waiting for transfers between devices, per_device(): group_rows = lax.all_gather(tokens, 'mlp', axis=0, tiled=True)  25 us
    reduce_scatter x1, waiting for transfers between devices, per_device(): lax.psum_scatter(down_terms.astype(jnp.bfloat16), 'mlp', scatter_dimensio...  24.9 us
    all_gather x1, waiting for transfers between devices, per_device(): lax.all_gather(w_gate, 'req', axis=0, tiled=True)  18.6 us
    dot_general x1, matrix products, fold_update(): jnp.einsum('rshd,rshv->rhdv', scaled, values.astype(jnp.float32), precisi...  8.54 us
    all_to_all x1, starting transfers between devices, per_device(): lax.all_to_all(jnp.take(fresh, send_order, axis=0).astype(jnp.bfloat16),...  6.87 us
  transfers between devices with their start and end apart: 7, of which 6 were waited for; matrix products, arithmetic and copies ran while one was open for 14% of the time, Pallas kernels for 0%

commit v1 on v0

--- a/solution.py
+++ b/solution.py
@@ -6,6 +6,22 @@
 
 DRAFT = 16
 epsilon = 1e-05
+
+
+def collect(x, axis, dim):
+    ways, here, step = (lax.axis_size(axis), lax.axis_index(axis), x.shape[dim])
+    lengths = [n * ways if d == dim else n for d, n in enumerate(x.shape)]
+    full = lax.dynamic_update_slice_in_dim(jnp.zeros(lengths, x.dtype), x, here * step, axis=dim)
+    going_up = going_down = x
+    for far in range(1, ways // 2 + 1):
+        going_up = lax.ppermute(going_up, axis, [(d, (d + 1) % ways) for d in range(ways)])
+        full = lax.dynamic_update_slice_in_dim(full, going_up, (here - far) % ways * step, axis=dim)
+        if 2 * far < ways:
+            going_down = lax.ppermute(going_down, axis, [(d, (d - 1) % ways) for d in range(ways)])
+            full = lax.dynamic_update_slice_in_dim(
+                full, going_down, (here + far) % ways * step, axis=dim
+            )
+    return full
 
 
 def layer_norm(inputs):
@@ -156,11 +172,7 @@
         preferred_element_type=jnp.float32,
     )
     hidden = (jax.nn.silu(gate_sum) * up_sum).astype(jnp.bfloat16)
-    down_terms = jnp.dot(
-        hidden,
-        lax.all_gather(w_down, "req", axis=1, tiled=True),
-        preferred_element_type=jnp.float32,
-    )
+    down_terms = jnp.dot(hidden, collect(w_down, "req", 1), preferred_element_type=jnp.float32)
     mixed = (
         residual_share
         + lax.psum_scatter(

time: 293 us -> 237 us (0.81)
  waiting for transfers between devices: 206 us -> 99.6 us
  starting transfers between devices: 7.29 us -> 43.7 us
  local copies, waits for them, and re-layouts: 5.76 us -> 19.3 us
    all_gather x1 -> x0, waiting for transfers between devices: 48.6 us -> none  [per_device(): lax.all_gather(w_down, 'req', axis=1, tiled=True)]
    ppermute x0 -> x15, starting transfers between devices: none -> 38.9 us  [the longest x7 37.3 us: collect(): lax.ppermute(going_down, axis, [(d, (d - 1) % ways) for d in range(ways)])]
    psum x1, waiting for transfers between devices: 35.1 us -> 0.02 us  [per_device(): summed = lax.psum(partials.astype(jnp.bfloat16), 'mlp').astype(jnp.float32)]
    all_gather x1, waiting for transfers between devices: 51.2 us -> 16.8 us  [per_device(): lax.all_gather(w_up, 'req', axis=0, tiled=True)]
    ppermute x0 -> x15, waiting for transfers between devices: none -> 20.6 us  [the longest x8 11.9 us: collect(): lax.ppermute(going_up, axis, [(d, (d + 1) % ways) for d in range(ways)])]
    all_gather x1, waiting for transfers between devices: 18.6 us -> 0.02 us  [per_device(): lax.all_gather(w_gate, 'req', axis=0, tiled=True)]
    all_to_all x1, waiting for transfers between devices: 0.01 us -> 17.8 us  [per_device(): lax.all_to_all(jnp.take(fresh, send_order, axis=0).astype(jnp.bfloat16),...]
    dynamic_update_slice x0 -> x16, local copies, waits for them, and re-layouts: none -> 12.7 us  [the longest x8 6.33 us: collect(): lax.dynamic_update_slice_in_dim(full, going_up, (here - far) % ways * ste...]
  transfers between devices with their start and end apart: 7 -> 21, of which waited for: 6 -> 14; matrix products, arithmetic and copies ran while one was open for 14% -> 23% of each run, Pallas kernels for 0% -> 0%
where the time goes in v1:
time: 237 us
  waiting for transfers between devices  99.6 us (42%)
  starting transfers between devices  43.7 us (18%)
  matrix products  32.1 us (14%)
  other arithmetic  26 us (11%)
  local copies, waits for them, and re-layouts  19.3 us (8%)
  between operations  15.9 us (7%)
    ppermute x7, starting transfers between devices, collect(): lax.ppermute(going_down, axis, [(d, (d - 1) % ways) for d in range(ways)])  37.3 us
    all_gather x1, waiting for transfers between devices, per_device(): group_rows = lax.all_gather(tokens, 'mlp', axis=0, tiled=True)  25.1 us
    reduce_scatter x1, waiting for transfers between devices, per_device(): lax.psum_scatter(down_terms.astype(jnp.bfloat16), 'mlp', scatter_dimensio...  17.9 us
    all_to_all x1, waiting for transfers between devices, per_device(): lax.all_to_all(jnp.take(fresh, send_order, axis=0).astype(jnp.bfloat16),...  17.8 us
    all_gather x1, waiting for transfers between devices, per_device(): lax.all_gather(w_up, 'req', axis=0, tiled=True)  16.8 us
    ppermute x8, waiting for transfers between devices, collect(): lax.ppermute(going_up, axis, [(d, (d + 1) % ways) for d in range(ways)])  11.9 us
    ppermute x7, waiting for transfers between devices, collect(): lax.ppermute(going_down, axis, [(d, (d - 1) % ways) for d in range(ways)])  8.65 us
    dot_general x1, matrix products, fold_update(): jnp.einsum('rshd,rshv->rhdv', scaled, values.astype(jnp.float32), precisi...  8.54 us
  transfers between devices with their start and end apart: 21, of which 14 were waited for; matrix products, arithmetic and copies ran while one was open for 23% of the time, Pallas kernels for 0%

profile of v1, /device:TPU:0, one launch (start us, length us, event | category | flops | bytes accessed | tf_op | source)
XLA Modules:
  0.0 236.5 jit_solution(13421337423239378367)
XLA Ops:
  8.1 0.7 all-gather.4.cloned.1.call-update
  8.9 1.2 convert_add_fusion.1
  10.1 0.7 add_convert_fusion.1
  10.8 0.7 power_select_fusion
  11.5 25.1 %all-gather.4.cloned.1.call-done = bf16[256,2048]{1,0:T(8,128)(2,1)} async-done(((bf16[32,2048]{1,0:T(8,128)(2,1)}), bf16[256,2048]{1,0:T(8,128)(2,1)}) %all-gather.4.cloned.1.call-update) | async-done | bytes 1048592 | tf_op jit(solution)/shard_map/all_gather | solution.py:122
  36.6 1.6 convert_reduce_fusion
  38.3 2.0 fusion.7
  40.2 2.0 fusion.62
  42.3 2.0 convolution_multiply_fusion.1
  44.3 0.6 fusion.46
  45.0 3.7 %fusion.14 = f32[16,1,512,16]{2,3,0,1:T(8,128)} fusion(f32[16,1,256,512]{3,2,1,0:T(8,128)S(1)} %copy-done.1, f32[16]{0:T(128)S(1)} %add_power_fusion, bf16[16,16,128]{2,1,0:T(8,128)(2,1)S(1)} %get-tuple-element.10, bf16[16,16,128]{2,1,0:T(8,128)(2,1)S(1)} %get-tuple-element.11), kind=kOutput, calls=%fused_computation.25 | convolution fusion | flops 403046400 | bytes 9044032 | tf_op jit(solution)/shard_map/rthd,rhdv->rthv/dot_general | solution.py:86
  48.7 0.8 convolution_convert_fusion.2
  49.4 2.2 fusion.65
  51.7 1.2 multiply_reduce_fusion.1
  53.0 2.4 %fusion.59 = f32[256,512]{1,0:T(8,128)S(1)} fusion(bf16[2048,512]{1,0:T(8,128)(2,1)} %param.21, bf16[256,2048]{1,0:T(8,128)(2,1)S(1)} %copy-done.2, f32[256]{0:T(256)} %copy-done.11, f32[256]{0:T(256)} %copy-done.9), kind=kOutput, calls=%fused_computation.118 | convolution fusion | flops 538968064 | bytes 3672064 | tf_op jit(solution)/shard_map/dot_general | solution.py:136
  55.4 0.2 multiply_convert_fusion.1
  55.6 1.8 convolution_convert_fusion.1
  57.5 0.5 all-gather.6.cloned.1.call-update
  58.1 1.6 collective-permute-start
  59.6 3.9 %collective-permute-start.1 = (bf16[512,128]{1,0:T(8,128)(2,1)}, bf16[512,128]{1,0:T(8,128)(2,1)}, u32[]{:S(2)}, u32[]{:S(2)}) collective-permute-start(bf16[512,128]{1,0:T(8,128)(2,1)} %param.25), channel_id=1, source_target_pairs={{0,120},{8,0},{16,8},{24,16},{32,24},{40,32},{48,40},{56,48},{64,5... | collective-permute-start | bytes 393224 | tf_op jit(solution)/shard_map/ppermute | solution.py:20
  64.0 1.6 broadcast_in_dim.22
  65.6 0.7 constant_dynamic-update-slice_fusion.15
  66.3 1.1 collective-permute-done
  67.5 5.3 %collective-permute-start.3 = (bf16[512,128]{1,0:T(8,128)(2,1)}, bf16[512,128]{1,0:T(8,128)(2,1)S(1)}, u32[]{:S(2)}, u32[]{:S(2)}) collective-permute-start(bf16[512,128]{1,0:T(8,128)(2,1)} %collective-permute-done.1), channel_id=1, source_target_pairs={{0,120},{8,0},{16,8},{24,16},{32,24},{40,32},{48,40},{56,48},{64,5... | collective-permute-start | bytes 393224 | tf_op jit(solution)/shard_map/ppermute | solution.py:20
  72.8 1.6 constant_dynamic-update-slice_fusion.14
  74.4 1.6 constant_dynamic-update-slice_fusion.13
  76.1 5.4 %collective-permute-start.5 = (bf16[512,128]{1,0:T(8,128)(2,1)S(1)}, bf16[512,128]{1,0:T(8,128)(2,1)S(1)}, u32[]{:S(2)}, u32[]{:S(2)}) collective-permute-start(bf16[512,128]{1,0:T(8,128)(2,1)S(1)} %collective-permute-done.3), channel_id=1, source_target_pairs={{0,120},{8,0},{16,8},{24,16},{32,24},{40,32},{48,40},{56,48},{64,5... | collective-permute-start | bytes 393224 | tf_op jit(solution)/shard_map/ppermute | solution.py:20
  81.5 0.7 constant_dynamic-update-slice_fusion.12
  82.2 0.7 constant_dynamic-update-slice_fusion.11
  82.8 1.9 collective-permute-done.4
  84.8 5.3 %collective-permute-start.7 = (bf16[512,128]{1,0:T(8,128)(2,1)S(1)}, bf16[512,128]{1,0:T(8,128)(2,1)S(1)}, u32[]{:S(2)}, u32[]{:S(2)}) collective-permute-start(bf16[512,128]{1,0:T(8,128)(2,1)S(1)} %collective-permute-done.5), channel_id=1, source_target_pairs={{0,120},{8,0},{16,8},{24,16},{32,24},{40,32},{48,40},{56,48},{64,5... | collective-permute-start | bytes 393224 | tf_op jit(solution)/shard_map/ppermute | solution.py:20
  90.1 0.7 constant_dynamic-update-slice_fusion.10
  90.8 0.7 constant_dynamic-update-slice_fusion.9
  91.5 1.6 collective-permute-done.6
  93.1 2.0 collective-permute-done.7
  95.1 5.8 %collective-permute-start.9 = (bf16[512,128]{1,0:T(8,128)(2,1)S(1)}, bf16[512,128]{1,0:T(8,128)(2,1)S(1)}, u32[]{:S(2)}, u32[]{:S(2)}) collective-permute-start(bf16[512,128]{1,0:T(8,128)(2,1)S(1)} %collective-permute-done.7), channel_id=1, source_target_pairs={{0,120},{8,0},{16,8},{24,16},{32,24},{40,32},{48,40},{56,48},{64,5... | collective-permute-start | bytes 393224 | tf_op jit(solution)/shard_map/ppermute | solution.py:20
  100.9 0.7 constant_dynamic-update-slice_fusion.8
  101.6 0.7 constant_dynamic-update-slice_fusion.7
  102.4 4.0 %collective-permute-done.9 = bf16[512,128]{1,0:T(8,128)(2,1)S(1)} collective-permute-done((bf16[512,128]{1,0:T(8,128)(2,1)S(1)}, bf16[512,128]{1,0:T(8,128)(2,1)S(1)}, u32[]{:S(2)}, u32[]{:S(2)}) %collective-permute-start.9) | collective-permute-done | bytes 131104 | tf_op jit(solution)/shard_map/ppermute | solution.py:20
  106.5 5.8 %collective-permute-start.11 = (bf16[512,128]{1,0:T(8,128)(2,1)S(1)}, bf16[512,128]{1,0:T(8,128)(2,1)S(1)}, u32[]{:S(2)}, u32[]{:S(2)}) collective-permute-start(bf16[512,128]{1,0:T(8,128)(2,1)S(1)} %collective-permute-done.9), channel_id=1, source_target_pairs={{0,120},{8,0},{16,8},{24,16},{32,24},{40,32},{48,40},{56,48},{64,5... | collective-permute-start | bytes 393224 | tf_op jit(solution)/shard_map/ppermute | solution.py:20
  112.3 0.7 constant_dynamic-update-slice_fusion.6
  113.0 0.7 constant_dynamic-update-slice_fusion.5
  113.7 2.1 collective-permute-done.11
  115.8 5.8 %collective-permute-start.13 = (bf16[512,128]{1,0:T(8,128)(2,1)S(1)}, bf16[512,128]{1,0:T(8,128)(2,1)S(1)}, u32[]{:S(2)}, u32[]{:S(2)}) collective-permute-start(bf16[512,128]{1,0:T(8,128)(2,1)S(1)} %collective-permute-done.11), channel_id=1, source_target_pairs={{0,120},{8,0},{16,8},{24,16},{32,24},{40,32},{48,40},{56,48},{64,5... | collective-permute-start | bytes 393224 | tf_op jit(solution)/shard_map/ppermute | solution.py:20
  121.6 0.7 constant_dynamic-update-slice_fusion.4
  122.2 0.7 constant_dynamic-update-slice_fusion.3
  122.9 0.7 constant_dynamic-update-slice_fusion.2
  123.6 0.5 collective-permute-done.13
  124.1 0.7 constant_dynamic-update-slice_fusion.1
  124.8 6.9 %collective-permute-done.14 = bf16[512,128]{1,0:T(8,128)(2,1)S(1)} collective-permute-done((bf16[512,128]{1,0:T(8,128)(2,1)S(1)}, bf16[512,128]{1,0:T(8,128)(2,1)S(1)}, u32[]{:S(2)}, u32[]{:S(2)}) %collective-permute-start.14) | collective-permute-done | bytes 131104 | tf_op jit(solution)/shard_map/ppermute | solution.py:17
  131.7 0.7 constant_dynamic-update-slice_fusion
  132.4 8.5 %fusion.1 = bf16[16,256,512]{2,1,0:T(8,128)(2,1)} fusion(f32[16,1,256,512]{3,2,1,0:T(8,128)} %param.14, f32[16]{0:T(128)S(1)} %copy-done.10, bf16[16,16,512]{2,1,0:T(8,128)(2,1)S(1)} %bitcast.68, f32[16,16]{1,0:T(8,128)S(1)} %copy-done.8, bf16[16,16,128]{2,1,0:T(8,128)(2,1)S(1)} %get-tuple-element.7, bf16[16,16,128]{2,1,0:T(8,128)(2,1)S(1)} %get-tuple-element.6), kind=kOutput, calls=%fused_computation.4 | convolution fusion | flops 409272320 | bytes 12977216 | tf_op jit(solution)/shard_map/rshd,rshv->rhdv/dot_general | solution.py:71
  140.9 4.9 %gather_fusion = bf16[16,256,512]{2,1,0:T(8,128)(2,1)} fusion(bf16[16,256,512]{2,1,0:T(8,128)(2,1)} %fusion.1, s32[1024]{0:T(1024)S(1)} %pad_clamp_fusion), kind=kCustom, calls=%fused_computation | custom fusion | bytes 8388672 | tf_op jit(solution)/shard_map/jit(_take)/gather | solution.py:146
  145.9 5.6 %fusion.4 = bf16[16,1,256,512]{3,2,1,0:T(8,128)(2,1)} fusion(bf16[16,256,512]{2,1,0:T(8,128)(2,1)} %gather_fusion, pred[16]{0:T(512)(128)(4,1)S(1)} %compare_and_fusion), kind=kLoop, calls=%fused_computation.8 | loop fusion | flops 2097152 | bytes 8388624 | tf_op jit(solution)/shard_map/convert_element_type | solution.py:146
  151.4 4.6 %all-to-all-start = ((bf16[16,1,256,512]{3,2,1,0:T(8,128)(2,1)}), bf16[16,1,256,512]{3,2,1,0:T(8,128)(2,1)}, u32[]{:S(2)}, u32[]{:S(2)}) async-start(bf16[16,1,256,512]{3,2,1,0:T(8,128)(2,1)} %fusion.4), calls=%async_computation.1 | async-start | bytes 8388608 | tf_op jit(solution)/shard_map/all_to_all | solution.py:145
  156.1 3.0 %convert_add_fusion = (f32[256,2048]{1,0:T(8,128)}, f32[256]{0:T(256)S(1)}) fusion(bf16[256,2048]{1,0:T(8,128)(2,1)S(1)} %copy-done.2, bf16[256,2048]{1,0:T(8,128)(2,1)} %all-reduce.2.cloned.1.call-done), kind=kLoop, calls=%fused_computation.9 | loop fusion | flops 2096896 | bytes 4195328 | tf_op jit(solution)/shard_map/add | solution.py:161
  159.1 0.5 multiply_reduce_fusion
  159.6 3.5 %fusion.58 = f32[256,512]{1,0:T(8,128)} fusion(bf16[2048,512]{1,0:T(8,128)(2,1)} %all-gather.6.cloned.1.call-done, f32[256]{0:T(256)S(1)} %add_rsqrt_fusion.1, f32[256]{0:T(256)S(1)} %broadcast_multiply_fusion.1, bf16[256,2048]{1,0:T(8,128)(2,1)} %all-reduce.2.cloned.1.call-done, bf16[256,2048]{1,0:T(8,128)(2,1)S(1)} %copy-done.2), kind=kOutput, calls=%fused_computation.117 | convolution fusion | flops 540016640 | bytes 4720640 | tf_op jit(solution)/shard_map/dot_general | solution.py:164
  163.1 16.8 %all-gather.8.cloned.1.call-done = bf16[2048,512]{1,0:T(8,128)(2,1)} async-done(((bf16[128,512]{1,0:T(8,128)(2,1)}), bf16[2048,512]{1,0:T(8,128)(2,1)}) %all-gather.8.cloned.1.call-update) | async-done | bytes 2097168 | tf_op jit(solution)/shard_map/all_gather | solution.py:171
  179.9 5.1 %convolution_convert_fusion = bf16[256,2048]{1,0:T(8,128)(2,1)} fusion(bf16[512,2048]{1,0:T(8,128)(2,1)} %constant_dynamic-update-slice_fusion, bf16[2048,512]{1,0:T(8,128)(2,1)} %all-gather.8.cloned.1.call-done, f32[256,512]{1,0:T(8,128)} %fusion.58, f32[256]{0:T(256)S(1)} %add_rsqrt_fusion.1, f32[256]{0:T(256)S(1)} %broadcast_multiply_fusion.1, ...), kind=kOutput, calls=%fused_computation.12 | convolution fusion | flops 1078198272 | bytes 7866368 | tf_op jit(solution)/shard_map/dot_general | solution.py:175
  185.1 17.8 %all-to-all-done = bf16[16,1,256,512]{3,2,1,0:T(8,128)(2,1)} async-done(((bf16[16,1,256,512]{3,2,1,0:T(8,128)(2,1)}), bf16[16,1,256,512]{3,2,1,0:T(8,128)(2,1)}, u32[]{:S(2)}, u32[]{:S(2)}) %all-to-all-start) | async-done | bytes 4194336 | tf_op jit(solution)/shard_map/all_to_all | solution.py:145
  202.9 6.8 %convert_element_type.101 = f32[16,1,256,512]{3,2,1,0:T(8,128)} convert(bf16[16,1,256,512]{3,2,1,0:T(8,128)(2,1)} %all-to-all-done) | non-fusion elementwise | flops 2097152 | bytes 12582912 | tf_op jit(solution)/shard_map/convert_element_type | solution.py:151
  209.8 17.9 %reduce-scatter.2.cloned.1.call-done = bf16[32,2048]{1,0:T(8,128)(2,1)} async-done(((bf16[256,2048]{1,0:T(8,128)(2,1)}), bf16[32,2048]{1,0:T(8,128)(2,1)}) %reduce-scatter.2.cloned.1.call-update) | async-done | bytes 131088 | tf_op jit(solution)/shard_map/reduce_scatter | solution.py:178
  227.7 1.7 add_convert_fusion
  (65 shorter events, 0.9 us)
Async XLA Ops:
  8.0 47.6 %copy-start = (bf16[512,2048]{1,0:T(8,128)(2,1)S(1)}, bf16[512,2048]{1,0:T(8,128)(2,1)}, u32[]{:S(2)}) copy-start(bf16[512,2048]{1,0:T(8,128)(2,1)} %param.22) | copy-start | bytes 6291460
  8.0 28.6 %all-gather.4.cloned.1.call-start = ((), (), s32[]{:S(2)}) async-start(), calls=%async_computation.2 | async-start | bytes 1179648 | tf_op jit(solution)/shard_map/all_gather | solution.py:122
  8.7 147.3 %all-reduce.2.cloned.1.call-start = ((), (), s32[]{:S(2)}) async-start(), calls=%async_computation.3 | async-start | bytes 2097152 | tf_op jit(solution)/shard_map/psum | solution.py:160
  36.6 8.3 %copy-start.1 = (f32[16,1,256,512]{3,2,1,0:T(8,128)S(1)}, f32[16,1,256,512]{3,2,1,0:T(8,128)}, u32[]{:S(2)}) copy-start(f32[16,1,256,512]{3,2,1,0:T(8,128)} %param.14) | copy-start | bytes 25165828
  38.2 10.4 %copy-start.9 = (f32[256]{0:T(256)}, f32[256]{0:T(256)S(1)}, u32[]{:S(2)}) copy-start(f32[256]{0:T(256)S(1)} %broadcast_multiply_fusion.2) | copy-start | bytes 3076
  40.2 8.4 %copy-start.11 = (f32[256]{0:T(256)}, f32[256]{0:T(256)S(1)}, u32[]{:S(2)}) copy-start(f32[256]{0:T(256)S(1)} %add_rsqrt_fusion.2) | copy-start | bytes 3076
  44.9 3.7 %copy-start.5 = (bf16[16,16,128]{2,1,0:T(8,128)(2,1)}, bf16[16,16,128]{2,1,0:T(8,128)(2,1)S(1)}, u32[]{:S(2)}) copy-start(bf16[16,16,128]{2,1,0:T(8,128)(2,1)S(1)} %get-tuple-element.10) | copy-start | bytes 196612
  44.9 3.7 %copy-start.6 = (bf16[16,16,128]{2,1,0:T(8,128)(2,1)}, bf16[16,16,128]{2,1,0:T(8,128)(2,1)S(1)}, u32[]{:S(2)}) copy-start(bf16[16,16,128]{2,1,0:T(8,128)(2,1)S(1)} %get-tuple-element.11) | copy-start | bytes 196612
  45.0 3.7 %copy-start.2 = (bf16[256,2048]{1,0:T(8,128)(2,1)S(1)}, bf16[256,2048]{1,0:T(8,128)(2,1)}, u32[]{:S(2)}) copy-start(bf16[256,2048]{1,0:T(8,128)(2,1)} %all-gather.4.cloned.1.call-done) | copy-start | bytes 3145732
  45.0 3.7 %copy-start.12 = (bf16[2048,512]{1,0:T(8,128)(2,1)S(1)}, bf16[2048,512]{1,0:T(8,128)(2,1)}, u32[]{:S(2)}) copy-start(bf16[2048,512]{1,0:T(8,128)(2,1)} %param.20) | copy-start | bytes 6291460
  52.9 2.4 %copy-start.3 = (f32[16,16,1,512]{3,1,0,2:T(8,128)S(1)}, f32[16,16,1,512]{3,1,0,2:T(8,128)}, u32[]{:S(2)}) copy-start(f32[16,16,1,512]{3,1,0,2:T(8,128)} %get-tuple-element.15) | copy-start | bytes 1572868
  55.6 7.9 %copy-start.13 = (s32[16]{0:T(128)S(1)}, s32[16]{0:T(128)}, u32[]{:S(2)}) copy-start(s32[16]{0:T(128)} %param.17) | copy-start | bytes 196
  57.4 102.2 %all-gather.6.cloned.1.call-start = ((), (), s32[]{:S(2)}) async-start(), calls=%async_computation.4 | async-start | bytes 2228224 | tf_op jit(solution)/shard_map/all_gather | solution.py:166
  58.0 121.9 %all-gather.8.cloned.1.call-start = ((), (), s32[]{:S(2)}) async-start(), calls=%async_computation.5 | async-start | bytes 2228224 | tf_op jit(solution)/shard_map/all_gather | solution.py:171
  58.1 9.4 %collective-permute-start = (bf16[512,128]{1,0:T(8,128)(2,1)}, bf16[512,128]{1,0:T(8,128)(2,1)}, u32[]{:S(2)}, u32[]{:S(2)}) collective-permute-start(bf16[512,128]{1,0:T(8,128)(2,1)} %param.25), channel_id=1, source_target_pairs={{0,8},{8,16},{16,24},{24,32},{32,40},{40,48},{48,56},{56,64},{64,7... | collective-permute-start | bytes 393224 | tf_op jit(solution)/shard_map/ppermute | solution.py:17
  59.6 7.8 %collective-permute-start.1 = (bf16[512,128]{1,0:T(8,128)(2,1)}, bf16[512,128]{1,0:T(8,128)(2,1)}, u32[]{:S(2)}, u32[]{:S(2)}) collective-permute-start(bf16[512,128]{1,0:T(8,128)(2,1)} %param.25), channel_id=1, source_target_pairs={{0,120},{8,0},{16,8},{24,16},{32,24},{40,32},{48,40},{56,48},{64,5... | collective-permute-start | bytes 393224 | tf_op jit(solution)/shard_map/ppermute | solution.py:20
  64.0 1.6 copy-start.7
  65.6 66.8 %copy-start.8 = (f32[16,16]{1,0:T(8,128)S(1)}, f32[16,16]{1,0:T(8,128)}, u32[]{:S(2)}) copy-start(f32[16,16]{1,0:T(8,128)} %get-tuple-element.16) | copy-start | bytes 3076
  65.6 66.8 %copy-start.10 = (f32[16]{0:T(128)S(1)}, f32[16]{0:T(128)}, u32[]{:S(2)}) copy-start(f32[16]{0:T(128)} %get-tuple-element.13) | copy-start | bytes 196
  67.5 8.7 %collective-permute-start.2 = (bf16[512,128]{1,0:T(8,128)(2,1)}, bf16[512,128]{1,0:T(8,128)(2,1)S(1)}, u32[]{:S(2)}, u32[]{:S(2)}) collective-permute-start(bf16[512,128]{1,0:T(8,128)(2,1)} %collective-permute-done), channel_id=1, source_target_pairs={{0,8},{8,16},{16,24},{24,32},{32,40},{40,48},{48,56},{56,64},{64,7... | collective-permute-start | bytes 393224 | tf_op jit(solution)/shard_map/ppermute | solution.py:17
  67.5 8.7 %collective-permute-start.3 = (bf16[512,128]{1,0:T(8,128)(2,1)}, bf16[512,128]{1,0:T(8,128)(2,1)S(1)}, u32[]{:S(2)}, u32[]{:S(2)}) collective-permute-start(bf16[512,128]{1,0:T(8,128)(2,1)} %collective-permute-done.1), channel_id=1, source_target_pairs={{0,120},{8,0},{16,8},{24,16},{32,24},{40,32},{48,40},{56,48},{64,5... | collective-permute-start | bytes 393224 | tf_op jit(solution)/shard_map/ppermute | solution.py:20
  76.1 8.6 %collective-permute-start.4 = (bf16[512,128]{1,0:T(8,128)(2,1)S(1)}, bf16[512,128]{1,0:T(8,128)(2,1)S(1)}, u32[]{:S(2)}, u32[]{:S(2)}) collective-permute-start(bf16[512,128]{1,0:T(8,128)(2,1)S(1)} %collective-permute-done.2), channel_id=1, source_target_pairs={{0,8},{8,16},{16,24},{24,32},{32,40},{40,48},{48,56},{56,64},{64,7... | collective-permute-start | bytes 393224 | tf_op jit(solution)/shard_map/ppermute | solution.py:17
  76.1 8.6 %collective-permute-start.5 = (bf16[512,128]{1,0:T(8,128)(2,1)S(1)}, bf16[512,128]{1,0:T(8,128)(2,1)S(1)}, u32[]{:S(2)}, u32[]{:S(2)}) collective-permute-start(bf16[512,128]{1,0:T(8,128)(2,1)S(1)} %collective-permute-done.3), channel_id=1, source_target_pairs={{0,120},{8,0},{16,8},{24,16},{32,24},{40,32},{48,40},{56,48},{64,5... | collective-permute-start | bytes 393224 | tf_op jit(solution)/shard_map/ppermute | solution.py:20
  84.8 8.3 %collective-permute-start.6 = (bf16[512,128]{1,0:T(8,128)(2,1)S(1)}, bf16[512,128]{1,0:T(8,128)(2,1)S(1)}, u32[]{:S(2)}, u32[]{:S(2)}) collective-permute-start(bf16[512,128]{1,0:T(8,128)(2,1)S(1)} %collective-permute-done.4), channel_id=1, source_target_pairs={{0,8},{8,16},{16,24},{24,32},{32,40},{40,48},{48,56},{56,64},{64,7... | collective-permute-start | bytes 393224 | tf_op jit(solution)/shard_map/ppermute | solution.py:17
  84.8 10.3 %collective-permute-start.7 = (bf16[512,128]{1,0:T(8,128)(2,1)S(1)}, bf16[512,128]{1,0:T(8,128)(2,1)S(1)}, u32[]{:S(2)}, u32[]{:S(2)}) collective-permute-start(bf16[512,128]{1,0:T(8,128)(2,1)S(1)} %collective-permute-done.5), channel_id=1, source_target_pairs={{0,120},{8,0},{16,8},{24,16},{32,24},{40,32},{48,40},{56,48},{64,5... | collective-permute-start | bytes 393224 | tf_op jit(solution)/shard_map/ppermute | solution.py:20
  93.1 9.4 %collective-permute-start.8 = (bf16[512,128]{1,0:T(8,128)(2,1)S(1)}, bf16[512,128]{1,0:T(8,128)(2,1)S(1)}, u32[]{:S(2)}, u32[]{:S(2)}) collective-permute-start(bf16[512,128]{1,0:T(8,128)(2,1)S(1)} %collective-permute-done.6), channel_id=1, source_target_pairs={{0,8},{8,16},{16,24},{24,32},{32,40},{40,48},{48,56},{56,64},{64,7... | collective-permute-start | bytes 393224 | tf_op jit(solution)/shard_map/ppermute | solution.py:17
  95.1 11.4 %collective-permute-start.9 = (bf16[512,128]{1,0:T(8,128)(2,1)S(1)}, bf16[512,128]{1,0:T(8,128)(2,1)S(1)}, u32[]{:S(2)}, u32[]{:S(2)}) collective-permute-start(bf16[512,128]{1,0:T(8,128)(2,1)S(1)} %collective-permute-done.7), channel_id=1, source_target_pairs={{0,120},{8,0},{16,8},{24,16},{32,24},{40,32},{48,40},{56,48},{64,5... | collective-permute-start | bytes 393224 | tf_op jit(solution)/shard_map/ppermute | solution.py:20
  102.4 11.2 %collective-permute-start.10 = (bf16[512,128]{1,0:T(8,128)(2,1)S(1)}, bf16[512,128]{1,0:T(8,128)(2,1)S(1)}, u32[]{:S(2)}, u32[]{:S(2)}) collective-permute-start(bf16[512,128]{1,0:T(8,128)(2,1)S(1)} %collective-permute-done.8), channel_id=1, source_target_pairs={{0,8},{8,16},{16,24},{24,32},{32,40},{40,48},{48,56},{56,64},{64,7... | collective-permute-start | bytes 393224 | tf_op jit(solution)/shard_map/ppermute | solution.py:17
  106.5 9.3 %collective-permute-start.11 = (bf16[512,128]{1,0:T(8,128)(2,1)S(1)}, bf16[512,128]{1,0:T(8,128)(2,1)S(1)}, u32[]{:S(2)}, u32[]{:S(2)}) collective-permute-start(bf16[512,128]{1,0:T(8,128)(2,1)S(1)} %collective-permute-done.9), channel_id=1, source_target_pairs={{0,120},{8,0},{16,8},{24,16},{32,24},{40,32},{48,40},{56,48},{64,5... | collective-permute-start | bytes 393224 | tf_op jit(solution)/shard_map/ppermute | solution.py:20
  113.6 9.3 %collective-permute-start.12 = (bf16[512,128]{1,0:T(8,128)(2,1)S(1)}, bf16[512,128]{1,0:T(8,128)(2,1)S(1)}, u32[]{:S(2)}, u32[]{:S(2)}) collective-permute-start(bf16[512,128]{1,0:T(8,128)(2,1)S(1)} %collective-permute-done.10), channel_id=1, source_target_pairs={{0,8},{8,16},{16,24},{24,32},{32,40},{40,48},{48,56},{56,64},{64,7... | collective-permute-start | bytes 393224 | tf_op jit(solution)/shard_map/ppermute | solution.py:17
  115.8 8.3 %collective-permute-start.13 = (bf16[512,128]{1,0:T(8,128)(2,1)S(1)}, bf16[512,128]{1,0:T(8,128)(2,1)S(1)}, u32[]{:S(2)}, u32[]{:S(2)}) collective-permute-start(bf16[512,128]{1,0:T(8,128)(2,1)S(1)} %collective-permute-done.11), channel_id=1, source_target_pairs={{0,120},{8,0},{16,8},{24,16},{32,24},{40,32},{48,40},{56,48},{64,5... | collective-permute-start | bytes 393224 | tf_op jit(solution)/shard_map/ppermute | solution.py:20
  122.9 8.8 %collective-permute-start.14 = (bf16[512,128]{1,0:T(8,128)(2,1)S(1)}, bf16[512,128]{1,0:T(8,128)(2,1)S(1)}, u32[]{:S(2)}, u32[]{:S(2)}) collective-permute-start(bf16[512,128]{1,0:T(8,128)(2,1)S(1)} %collective-permute-done.12), channel_id=1, source_target_pairs={{0,8},{8,16},{16,24},{24,32},{32,40},{40,48},{48,56},{56,64},{64,7... | collective-permute-start | bytes 393224 | tf_op jit(solution)/shard_map/ppermute | solution.py:17
  151.4 51.5 %all-to-all-start = ((bf16[16,1,256,512]{3,2,1,0:T(8,128)(2,1)}), bf16[16,1,256,512]{3,2,1,0:T(8,128)(2,1)}, u32[]{:S(2)}, u32[]{:S(2)}) async-start(bf16[16,1,256,512]{3,2,1,0:T(8,128)(2,1)} %fusion.4), calls=%async_computation.1 | async-start | bytes 8388608 | tf_op jit(solution)/shard_map/all_to_all | solution.py:145
  156.0 71.7 %reduce-scatter.2.cloned.1.call-start = ((), (), s32[]{:S(2)}) async-start(), calls=%async_computation.6 | async-start | bytes 1179648 | tf_op jit(solution)/shard_map/reduce_scatter | solution.py:178
  156.1 3.0 %copy-start.4 = (bf16[256,2048]{1,0:T(8,128)(2,1)S(1)}, bf16[256,2048]{1,0:T(8,128)(2,1)}, u32[]{:S(2)}) copy-start(bf16[256,2048]{1,0:T(8,128)(2,1)} %all-reduce.2.cloned.1.call-done) | copy-start | bytes 3145732
Sparse Core Ops, SparseCore 0:
  10.6 26.0 all-gather.3
  57.6 63.3 all-reduce.1
  185.2 42.4 reduce-scatter.1
Sparse Core Ops, SparseCore 1:
  60.1 48.3 all-gather.5
  110.4 69.5 all-gather.7
